TPU v7x, 128 devices: a whole 4x4x4 slice. The times are simulated.
128 devices in a mesh: aux: 32 (over x, y, core), pair: 4 (over z).
Axes of the slice: x: 4, y: 4, z: 4, core: 2. Of those that a mesh axis runs over, the one named last changes fastest.
Arguments:
- three_center: bfloat16 [8, 32, 32, 8192], P('pair', None, None, 'aux'), may hold values from -6 to 6
- pair_index: int32 [2, 8], replicated, may hold values from 0 to 31, as said below
- green_occ: bfloat16 [1024, 1024], replicated, may hold values from -0.0625 to 0.0625
- green_virt: bfloat16 [1024, 1024], replicated, may hold values from -0.0625 to 0.0625
- coupling: int32 [32, 32], replicated, may hold values 0 or 1
Outputs:
- polarizability: float32 [8192, 8192], P('aux', 'pair')
Inputs may be any that keep to these rules, and one draw needn't show every extreme that they name: The 8 pairs (pair_index[0, k], pair_index[1, k]) are distinct block pairs.
All inputs are finite; a program needn't handle non-finite values.
Results may differ from a plain program's by a relative error of at most 0.015.
Values may be sent and summed in bfloat16 or wider, within the bound.
A program may use at most 128 MiB of HBM per device.

v0:
```python
import jax
import jax.numpy as jnp
from jax import lax
from jax.sharding import PartitionSpec as P


def block_of(matrix, row_block, column_block, block_width):
    return lax.dynamic_slice(
        matrix, (row_block * block_width, column_block * block_width), (block_width, block_width)
    )


def block_term(tensor_block, occ_block, virt_block, active):
    block_width = tensor_block.shape[0]
    aux_local = tensor_block.shape[2]

    def compute(operands):
        tensor_in, occ_in, virt_in = operands
        occupied = lax.dot_general(
            occ_in,
            tensor_in.reshape(block_width, block_width * aux_local),
            (((0,), (0,)), ((), ())),
            preferred_element_type=jnp.float32,
        ).astype(jnp.bfloat16)
        return jnp.einsum(
            "nlp,ls->nsp",
            occupied.reshape(block_width, block_width, aux_local),
            virt_in,
            preferred_element_type=jnp.float32,
        )

    def nothing(operands):
        return jnp.zeros((block_width, block_width, aux_local), jnp.float32)

    return lax.cond(active > 0, compute, nothing, (tensor_block, occ_block, virt_block))


def pair_term(tensor_block, source, target, pair_index, green_occ, green_virt, coupling):
    block_width = tensor_block.shape[0]
    source_row = pair_index[0, source]
    source_col = pair_index[1, source]
    target_row = pair_index[0, target]
    target_col = pair_index[1, target]
    active = coupling[source_row, target_row] * coupling[source_col, target_col]
    occ_block = block_of(green_occ, source_row, target_row, block_width)
    virt_block = block_of(green_virt, source_col, target_col, block_width)
    return block_term(tensor_block, occ_block, virt_block, active)


def on_device(three_center, pair_index, green_occ, green_virt, coupling):
    owned_count = three_center.shape[0]
    block_width = three_center.shape[1]
    aux_local = three_center.shape[3]
    first_owned = lax.axis_index("pair") * owned_count

    def for_target(offset):
        running_sum = jnp.zeros((block_width, block_width, aux_local), jnp.float32)
        for slot_number in range(owned_count):
            running_sum = running_sum + pair_term(
                three_center[slot_number],
                first_owned + slot_number,
                offset,
                pair_index,
                green_occ,
                green_virt,
                coupling,
            )
        return running_sum

    summed = lax.psum_scatter(
        lax.map(
            for_target, jnp.arange(owned_count * lax.axis_size("pair"), dtype=jnp.int32)
        ).astype(jnp.bfloat16),
        "pair",
        scatter_dimension=0,
        tiled=True,
    )
    contracted = summed.reshape(owned_count * block_width * block_width, aux_local)
    flat_tensor = three_center.reshape(owned_count * block_width * block_width, aux_local)
    partial_value = lax.dot_general(
        contracted,
        lax.all_gather(flat_tensor, "aux", axis=1, tiled=True),
        (((0,), (0,)), ((), ())),
        preferred_element_type=jnp.float32,
    )
    return lax.psum_scatter(
        partial_value.astype(jnp.bfloat16), "pair", scatter_dimension=1, tiled=True
    ).astype(jnp.float32)


def solution(mesh):
    placed = (P("pair", None, None, "aux"), P(), P(), P(), P())
    return jax.shard_map(
        on_device, mesh=mesh, in_specs=placed, out_specs=P("aux", "pair"), check_vma=False
    )
```

profile of v0, /device:TPU:1, one launch (start us, length us, event | category | flops | bytes accessed | tf_op | source)
XLA Modules:
  0.0 362.4 jit_solution(18079458189552463908)
XLA Ops:
  7.4 1.6 constant_dynamic-slice_fusion.2
  16.7 3.9 %copy.6 = bf16[1024,1024]{0,1:T(8,128)(2,1)} copy(bf16[1024,1024]{1,0:T(8,128)(2,1)} %param.14) | data formatting | bytes 4194304 | tf_op jit(solution)/shard_map/while | solution.py:71
  23.2 135.6 %while.12 = (s32[]{:T(128)}, bf16[8,32,32,256]{3,2,1,0:T(8,128)(2,1)}, s32[8]{0:T(128)S(1)}, s32[2,8]{1,0:T(2,128)S(1)}, s32[32,32]{1,0:T(8,128)}, /*index=5*/s3...) while((s32[]{:T(128)}, ...), condition=%wide.region_5.6_spmd, body=%wide.region_0.5_spmd.sunk | while | flops 67895312 | bytes 14718099 | solution.py:71
  31.7 1.5 fusion.14
  35.8 2.7 conditional.4
  36.2 1.1 convolution_convert_fusion
  37.5 1.1 convolution_bitcast_fusion
  48.0 1.5 fusion.14
  52.3 1.0 bitcast_dynamic-update-slice_fusion.2
  61.7 1.5 fusion.14
  64.4 2.7 conditional.5
  64.8 1.2 convolution_convert_fusion.1
  66.0 1.1 convolution_bitcast_fusion.1
  68.5 2.7 conditional.4
  68.8 1.2 convolution_convert_fusion
  70.1 1.1 convolution_bitcast_fusion
  80.6 1.5 fusion.14
  83.3 2.7 conditional.5
  83.7 1.1 convolution_convert_fusion.1
  85.0 1.1 convolution_bitcast_fusion.1
  87.4 2.7 conditional.4
  87.7 1.1 convolution_convert_fusion
  89.0 1.1 convolution_bitcast_fusion
  99.5 1.5 fusion.14
  102.2 2.7 conditional.5
  102.6 1.1 convolution_convert_fusion.1
  103.8 1.1 convolution_bitcast_fusion.1
  106.3 2.7 conditional.4
  106.6 1.1 convolution_convert_fusion
  107.9 1.1 convolution_bitcast_fusion
  118.4 1.5 fusion.14
  122.6 2.7 conditional.4
  122.9 1.1 convolution_convert_fusion
  124.2 1.1 convolution_bitcast_fusion
  134.7 1.5 fusion.14
  137.4 2.7 conditional.5
  137.7 1.1 convolution_convert_fusion.1
  139.0 1.1 convolution_bitcast_fusion.1
  141.4 2.7 conditional.4
  141.8 1.1 convolution_convert_fusion
  143.0 1.1 convolution_bitcast_fusion
  144.1 1.0 bitcast_dynamic-update-slice_fusion.2
  153.6 1.5 fusion.14
  159.5 47.0 %reduce-scatter.3.cloned.1.call-done = bf16[2,32,32,256]{3,2,1,0:T(8,128)(2,1)} async-done(((bf16[8,32,32,256]{3,2,1,0:T(8,128)(2,1)}), bf16[2,32,32,256]{3,2,1,0:T(8,128)(2,1)}) %reduce-scatter.3.cloned.1.call-update) | async-done | bytes 1048592 | tf_op jit(solution)/shard_map/reduce_scatter | solution.py:70
  206.5 81.1 %all-gather.2.cloned.1.call-done = bf16[2048,8192]{1,0:T(8,128)(2,1)} async-done(((bf16[2048,256]{1,0:T(8,128)(2,1)}), bf16[2048,8192]{1,0:T(8,128)(2,1)}) %all-gather.2.cloned.1.call-update) | async-done | bytes 33554448 | tf_op jit(solution)/shard_map/all_gather | solution.py:82
  287.6 16.8 %convolution_convert_fusion.2 = bf16[256,8192]{1,0:T(8,128)(2,1)} fusion(bf16[2048,256]{1,0:T(8,128)(2,1)} %bitcast.60, bf16[2048,8192]{1,0:T(8,128)(2,1)} %all-gather.2.cloned.1.call-done), kind=kOutput, calls=%fused_computation.13 | convolution fusion | flops 8592031744 | bytes 38797312 | tf_op jit(solution)/shard_map/dot_general | solution.py:80
  304.4 47.8 %reduce-scatter.5.cloned.1.call-done = bf16[256,2048]{1,0:T(8,128)(2,1)} async-done(((bf16[256,8192]{1,0:T(8,128)(2,1)}), bf16[256,2048]{1,0:T(8,128)(2,1)}) %reduce-scatter.5.cloned.1.call-update) | async-done | bytes 1048592 | tf_op jit(solution)/shard_map/reduce_scatter | solution.py:86
  352.2 2.8 convert_element_type.33
  (76 shorter events, 22.6 us)
Async XLA Ops:
  7.4 15.8 %copy-start.1 = (s32[2,8]{1,0:T(2,128)S(1)}, s32[2,8]{1,0:T(2,128)}, u32[]{:S(2)}) copy-start(s32[2,8]{1,0:T(2,128)} %param.12) | copy-start | bytes 196
  7.4 15.8 %copy-start = (bf16[2,32,32,256]{3,2,1,0:T(8,128)(2,1)S(1)}, bf16[2,32,32,256]{3,2,1,0:T(8,128)(2,1)}, u32[]{:S(2)}) copy-start(bf16[2,32,32,256]{3,2,1,0:T(8,128)(2,1)} %param.11) | copy-start | bytes 3145732
  7.4 199.1 %reduce-scatter.3.cloned.1.call-start = ((), (), s32[]{:S(2)}) async-start(), calls=%async_computation.2 | async-start | bytes 5242880 | tf_op jit(solution)/shard_map/reduce_scatter | solution.py:70
  158.9 128.7 %all-gather.2.cloned.1.call-start = ((), (), s32[]{:S(2)}) async-start(), calls=%async_computation.3 | async-start | bytes 34603008 | tf_op jit(solution)/shard_map/all_gather | solution.py:82
  159.4 192.8 %reduce-scatter.5.cloned.1.call-start = ((), (), s32[]{:S(2)}) async-start(), calls=%async_computation.4 | async-start | bytes 5242880 | tf_op jit(solution)/shard_map/reduce_scatter | solution.py:86
Sparse Core Ops, SparseCore 0:
  159.0 47.4 reduce-scatter.2
  304.5 47.6 reduce-scatter.4
Sparse Core Ops, SparseCore 1:
  161.7 125.8 all-gather.1
where the time goes:
time: 360 us; the launch traced here: 362 us
  waiting for transfers between devices  176 us (49%)
  loops' own time  78.6 us (22%)
  matrix products  39 us (11%)
  local copies, waits for them, and re-layouts  32.6 us (9%)
  between operations  25.2 us (7%)
  other arithmetic  10.6 us (3%)
    all_gather x1, waiting for transfers between devices, on_device(): lax.all_gather(flat_tensor, 'aux', axis=1, tiled=True)  81.1 us
    another operation x1, loops' own time, on_device(): lax.map(for_target, jnp.arange(owned_count * lax.axis_size('pair'), dtype...  77.9 us
    reduce_scatter x1, waiting for transfers between devices, on_device(): lax.psum_scatter(partial_value.astype(jnp.bfloat16), 'pair', scatter_dime...  47.8 us
    reduce_scatter x1, waiting for transfers between devices, on_device(): lax.psum_scatter(lax.map(for_target, jnp.arange(owned_count * lax.axis_si...  47 us
    dot_general x1, matrix products, on_device(): lax.dot_general(contracted, lax.all_gather(flat_tensor, 'aux', axis=1, ti...  16.8 us
    dynamic_slice x8, local copies, waits for them, and re-layouts, pair_term(): active = coupling[source_row, target_row] * coupling[source_col, target_col]  11.7 us
    dot_general x10, matrix products, compute(): lax.dot_general(occ_in, tensor_in.reshape(block_width, block_width * aux_...  11.4 us
    dot_general x10, matrix products, compute(): jnp.einsum('nlp,ls->nsp', occupied.reshape(block_width, block_width, aux_...  10.8 us
  transfers between devices with their start and end apart: 3, of which 3 were waited for; matrix products, arithmetic and copies ran while one was open for 0% of the time, Pallas kernels for 0%

commit v1 on v0

v1 whole, which is shorter than its diff:
```python
import functools

import jax
import jax.numpy as jnp
from jax import lax
from jax.experimental import pallas as pl
from jax.experimental.pallas import tpu as pltpu
from jax.sharding import PartitionSpec as P

MESH = pl.DeviceIdType.MESH
RING = 4
CHUNKS = 2
Y_OFFSET = (0, 3, 1, 2)


def polarizability_kernel(
    pair_ref, coup_ref, t_ref, occ_hbm, virt_hbm, o_ref,
    occ, virt, tz, tq, ee, vv, acc, ct, d_send, d_half, d_in, d_own, r_buf,
    send_sem, recv_sem, local_sem,
):
    kdim, width = t_ref.shape
    chunk = width // CHUNKS
    block = 32
    square = block * block
    half = kdim // 2
    n_pairs = pair_ref.shape[1]
    owned = n_pairs // RING

    aux = lax.axis_index("aux")
    z = lax.axis_index("pair")
    core = lax.rem(aux, 2)
    y = lax.rem(aux // 2, RING)
    x = aux // (2 * RING)

    def at_x(s):
        return {"aux": (lax.rem(x + s, RING) * RING + y) * 2 + core}

    def at_y(s):
        return {"aux": (x * RING + lax.rem(y + s, RING)) * 2 + core}

    def at_z(s):
        return {"pair": lax.rem(z + s, RING)}

    partner = {"aux": aux + 1 - 2 * core}

    counter = [0]

    def remote(src, dst, device):
        i = counter[0]
        counter[0] += 1
        return pltpu.make_async_remote_copy(
            src_ref=src, dst_ref=dst, send_sem=send_sem.at[i], recv_sem=recv_sem.at[i],
            device_id=device, device_id_type=MESH,
        )

    local_counter = [0]

    def local(src, dst):
        i = local_counter[0]
        local_counter[0] += 1
        return pltpu.make_async_copy(src, dst, local_sem.at[i])

    cols = [pl.ds(h * chunk, chunk) for h in range(CHUNKS)]
    z_plus = [remote(t_ref.at[:, cols[h]], tz.at[h, 0], at_z(1)) for h in range(CHUNKS)]
    z_minus = [remote(t_ref.at[:, cols[h]], tz.at[h, 1], at_z(3)) for h in range(CHUNKS)]
    lo, hi = pl.ds(0, half), pl.ds(half, half)
    zf_plus = [remote(tz.at[h, 0, lo], tz.at[h, 2, lo], at_z(1)) for h in range(CHUNKS)]
    zf_minus = [remote(tz.at[h, 1, hi], tz.at[h, 2, hi], at_z(3)) for h in range(CHUNKS)]

    x_plus = remote(t_ref, tq.at[3, core], at_x(1))
    x_minus = remote(t_ref, tq.at[1, core], at_x(3))
    xf_plus = remote(tq.at[3, core, lo], tq.at[2, core, lo], at_x(1))
    xf_minus = remote(tq.at[1, core, hi], tq.at[2, core, hi], at_x(3))
    core_copy = [remote(t_ref if o == 0 else tq.at[o, core], tq.at[o, core], partner) for o in range(RING)]

    def yrows(slot, part=0, parts=1):
        return pl.ds(slot * chunk + part * (chunk // parts), chunk // parts)

    y_plus = [remote(ct.at[h, yrows(0)], ct.at[h, yrows(1)], at_y(1)) for h in range(CHUNKS)]
    y_minus = [remote(ct.at[h, yrows(0)], ct.at[h, yrows(2)], at_y(3)) for h in range(CHUNKS)]
    yf_plus = [remote(ct.at[h, yrows(1, 0, 2)], ct.at[h, yrows(3, 0, 2)], at_y(1)) for h in range(CHUNKS)]
    yf_minus = [remote(ct.at[h, yrows(2, 1, 2)], ct.at[h, yrows(3, 1, 2)], at_y(3)) for h in range(CHUNKS)]

    half_plus = [remote(d_send.at[h, 1, 0], d_half.at[h, 0], at_z(1)) for h in range(CHUNKS)]
    half_minus = [remote(d_send.at[h, 1, 1], d_half.at[h, 1], at_z(3)) for h in range(CHUNKS)]
    d_plus = [[remote(d_send.at[h, 0, c], d_in.at[h, 0, c], at_z(1)) for c in range(2)] for h in range(CHUNKS)]
    d_minus = [[remote(d_send.at[h, 2, c], d_in.at[h, 1, c], at_z(3)) for c in range(2)] for h in range(CHUNKS)]

    wide = 2 * width
    ocols = pl.ds(pl.multiple_of(y * wide, wide), wide)
    out_copy = [
        [
            remote(r_buf.at[h, yrows(s)], o_ref.at[cols[h], ocols], at_y(Y_OFFSET[s]))
            for s in range(1, RING)
        ]
        for h in range(CHUNKS)
    ]
    out_own = [local(r_buf.at[h, yrows(0)], o_ref.at[cols[h], ocols]) for h in range(CHUNKS)]
    keep = local(t_ref, tq.at[0, core])
    load_occ = local(occ_hbm, occ)
    load_virt = local(virt_hbm, virt)

    load_occ.start()
    load_virt.start()
    keep.start()

    barrier = pltpu.get_barrier_semaphore()
    greeted = [at_x(1), at_x(3), at_y(1), at_y(2), at_y(3), at_z(1), at_z(3), partner]
    for device in greeted:
        pl.semaphore_signal(barrier, inc=1, device_id=device, device_id_type=MESH)
    pl.semaphore_wait(barrier, len(greeted))

    z_plus[0].start()
    z_minus[0].start()
    x_plus.start()
    x_minus.start()
    core_copy[0].start()

    load_occ.wait()
    load_virt.wait()

    def indices(which, positions):
        return [pair_ref[which, position] for position in positions]

    sources = range(n_pairs)
    targets = [z * owned + t for t in range(owned)]

    def onehot(starts, width, step):
        row = lax.broadcasted_iota(jnp.int32, (block, width), 0)
        offset = lax.broadcasted_iota(jnp.int32, (block, width), 1) - row * step
        parts = [(offset == start).astype(jnp.float32).astype(jnp.bfloat16) for start in starts]
        return jnp.concatenate(parts, axis=0)

    def outer(left, right):
        return lax.dot_general(left, right, (((1,), (1,)), ((), ())), preferred_element_type=jnp.float32)

    def select(matrix, which):
        size = matrix.shape[1]
        pick = onehot([i * block for i in indices(which, sources)], size, 1)
        rows = jnp.dot(pick, matrix[...], preferred_element_type=jnp.float32).astype(jnp.bfloat16)
        return outer(onehot([i * block for i in indices(which, targets)], size, 1), rows)

    coupling = coup_ref[...].astype(jnp.float32).astype(jnp.bfloat16)

    def kept(which):
        size = coupling.shape[1]
        pick = onehot(indices(which, sources), size, 0)
        rows = jnp.dot(pick, coupling, preferred_element_type=jnp.float32).astype(jnp.bfloat16)
        return outer(onehot(indices(which, targets), size, 0), rows)

    occ_t = (select(occ, 0) * kept(0) * kept(1)).astype(jnp.bfloat16)
    virt_t = select(virt, 1).astype(jnp.bfloat16)

    def expand(k, carry):
        row = lax.broadcasted_iota(jnp.int32, (n_pairs * block, square), 0)
        lane = lax.broadcasted_iota(jnp.int32, (n_pairs * block, square), 1)
        spread = (row == k * block + lane // block).astype(jnp.float32).astype(jnp.bfloat16)
        tiled = (row == k * block + lane % block).astype(jnp.float32).astype(jnp.bfloat16)
        ee[k] = jnp.dot(occ_t, spread, preferred_element_type=jnp.float32)
        vv[k] = jnp.dot(virt_t, tiled, preferred_element_type=jnp.float32)
        return carry

    lax.fori_loop(0, n_pairs, expand, 0)

    acc[...] = jnp.zeros_like(acc)

    def mix(h, source_z, load):
        def step(i, carry):
            kk = i // 8
            t = lax.rem(i // 4, 2)
            part = lax.rem(i, 4)
            k = source_z * owned + kk
            first = pl.multiple_of(t * block + part * 8, 8)
            left = ee[k, pl.ds(first, 8), :]
            right = vv[k, pl.ds(pl.multiple_of(t * block, block), block), :]
            rows = [(left[j : j + 1, :] * right).astype(jnp.bfloat16) for j in range(8)]
            matrix = jnp.concatenate(rows, axis=0)
            tensor = load(pl.ds(pl.multiple_of(kk * square, square), square))
            out = pl.ds(pl.multiple_of(part * 8 * block, 8 * block), 8 * block)
            acc[h, t, out, :] += jnp.dot(matrix, tensor, preferred_element_type=jnp.float32)
            return carry

        lax.fori_loop(0, owned * owned * 4, step, 0)

    def finish(h):
        for t in range(owned):
            ct[h, 0:chunk, t * square : (t + 1) * square] = acc[h, t].T.astype(jnp.bfloat16)

    for h in range(CHUNKS):
        mix(h, z, lambda rows, h=h: t_ref[rows, h * chunk : (h + 1) * chunk])

    def z_arrive(h):
        z_plus[h].wait_recv()
        zf_plus[h].start()
        z_minus[h].wait_recv()
        zf_minus[h].start()

    def mix_near(h):
        mix(h, lax.rem(z + 3, RING), lambda rows: tz[h, 0, rows, :])
        mix(h, lax.rem(z + 1, RING), lambda rows: tz[h, 1, rows, :])

    def mix_far(h):
        zf_plus[h].wait_recv()
        zf_minus[h].wait_recv()
        mix(h, lax.rem(z + 2, RING), lambda rows: tz[h, 2, rows, :])
        finish(h)
        y_plus[h].start()
        y_minus[h].start()

    def y_arrive(h):
        y_plus[h].wait_recv()
        yf_plus[h].start()
        y_minus[h].wait_recv()
        yf_minus[h].start()

    z_arrive(0)
    z_plus[1].start()
    z_minus[1].start()
    mix_near(0)
    mix_far(0)
    x_plus.wait_recv()
    xf_plus.start()
    core_copy[3].start()
    x_minus.wait_recv()
    xf_minus.start()
    core_copy[1].start()
    z_arrive(1)
    mix_near(1)
    y_arrive(0)
    mix_far(1)
    xf_plus.wait_recv()
    xf_minus.wait_recv()
    core_copy[2].start()
    keep.wait()
    yf_plus[0].wait_recv()
    yf_minus[0].wait_recv()
    for o in range(RING):
        core_copy[o].wait_recv()

    def product(h, r, store):
        o = lax.rem(z + r + RING - x, RING)

        def step(i, carry):
            c = i // 2
            rows = pl.ds(pl.multiple_of(lax.rem(i, 2) * (2 * chunk), 2 * chunk), 2 * chunk)
            store(c, rows, jnp.dot(ct[h, rows, :], tq[o, c], preferred_element_type=jnp.float32))
            return carry

        lax.fori_loop(0, 4, step, 0)

    def to_send(h, r):
        def store(c, rows, value):
            d_send[h, r - 1, c, rows, :] = value.astype(jnp.bfloat16)

        return store

    def join(h, r, c, j):
        total = d_send[h, r - 1, c].astype(jnp.float32) + d_half[h, j].astype(jnp.float32)
        d_send[h, r - 1, c] = total.astype(jnp.bfloat16)

    def reduce_start(h):
        product(h, 2, to_send(h, 2))
        half_plus[h].start()
        half_minus[h].start()
        product(h, 1, to_send(h, 1))
        d_plus[h][1].start()
        product(h, 3, to_send(h, 3))
        d_minus[h][0].start()
        half_plus[h].wait_recv()
        join(h, 1, 0, 0)
        d_plus[h][0].start()
        half_minus[h].wait_recv()
        join(h, 3, 1, 1)
        d_minus[h][1].start()

        def store(c, rows, value):
            d_own[h, c, rows, :] = value

        product(h, 0, store)

    def reduce_end(h):
        for c in range(2):
            d_plus[h][c].wait_recv()
            d_minus[h][c].wait_recv()
            total = d_own[h, c] + d_in[h, 0, c].astype(jnp.float32) + d_in[h, 1, c].astype(jnp.float32)
            r_buf[h, :, c * width : (c + 1) * width] = total.astype(jnp.bfloat16)
        for copy in out_copy[h]:
            copy.start()
        out_own[h].start()

    reduce_start(0)
    y_arrive(1)
    yf_plus[1].wait_recv()
    yf_minus[1].wait_recv()
    reduce_start(1)
    reduce_end(0)
    reduce_end(1)

    for h in range(CHUNKS):
        for copy in out_copy[h]:
            copy.wait_recv()
        out_own[h].wait()
    sends = [x_plus, x_minus, xf_plus, xf_minus] + core_copy
    for h in range(CHUNKS):
        sends += [z_plus[h], z_minus[h], zf_plus[h], zf_minus[h]]
        sends += [y_plus[h], y_minus[h], yf_plus[h], yf_minus[h]]
        sends += [half_plus[h], half_minus[h]] + d_plus[h] + d_minus[h] + out_copy[h]
    for copy in sends:
        copy.wait_send()


def on_device(three_center, pair_index, green_occ, green_virt, coupling):
    owned, block, _, width = three_center.shape
    kdim = owned * block * block
    chunk = width // CHUNKS
    rows = RING * chunk
    n_pairs = pair_index.shape[1]
    bf16, f32 = jnp.bfloat16, jnp.float32
    part = pl.pallas_call(
        polarizability_kernel,
        out_shape=jax.ShapeDtypeStruct((width, RING * 2 * width), bf16),
        in_specs=[
            pl.BlockSpec(memory_space=pltpu.SMEM),
            pl.BlockSpec(memory_space=pltpu.VMEM),
            pl.BlockSpec(memory_space=pltpu.VMEM),
            pl.BlockSpec(memory_space=pl.ANY),
            pl.BlockSpec(memory_space=pl.ANY),
        ],
        out_specs=pl.BlockSpec(memory_space=pl.ANY),
        scratch_shapes=[
            pltpu.VMEM(green_occ.shape, bf16),
            pltpu.VMEM(green_virt.shape, bf16),
            pltpu.VMEM((CHUNKS, 3, kdim, chunk), bf16),
            pltpu.VMEM((RING, 2, kdim, width), bf16),
            pltpu.VMEM((n_pairs, owned * block, block * block), f32),
            pltpu.VMEM((n_pairs, owned * block, block * block), f32),
            pltpu.VMEM((CHUNKS, owned, block * block, chunk), f32),
            pltpu.VMEM((CHUNKS, rows, kdim), bf16),
            pltpu.VMEM((CHUNKS, 3, 2, rows, width), bf16),
            pltpu.VMEM((CHUNKS, 2, rows, width), bf16),
            pltpu.VMEM((CHUNKS, 2, 2, rows, width), bf16),
            pltpu.VMEM((CHUNKS, 2, rows, width), f32),
            pltpu.VMEM((CHUNKS, rows, 2 * width), bf16),
            pltpu.SemaphoreType.DMA((48,)),
            pltpu.SemaphoreType.DMA((48,)),
            pltpu.SemaphoreType.DMA((5,)),
        ],
        compiler_params=pltpu.CompilerParams(
            collective_id=0, has_side_effects=True, vmem_limit_bytes=56 * 1024 * 1024
        ),
        name="polarizability",
    )(pair_index, coupling, three_center.reshape(kdim, width), green_occ, green_virt)
    return part.astype(f32)


def solution(mesh):
    placed = (P("pair", None, None, "aux"), P(), P(), P(), P())
    return jax.shard_map(
        on_device, mesh=mesh, in_specs=placed, out_specs=P("aux", "pair"), check_vma=False
    )
```

time: 360 us -> 110 us (0.31); the launches traced: 362 us -> 109 us
  waiting for transfers between devices: 176 us -> 0 us
  Pallas kernels: 0 us -> 106 us
  loops' own time: 78.6 us -> 0 us
  matrix products: 39 us -> 0 us
  local copies, waits for them, and re-layouts: 32.6 us -> 0 us
  between operations: 25.2 us -> 0.01 us
  other arithmetic: 10.6 us -> 2.79 us
    pallas_call x0 -> x1, Pallas kernels: none -> 106 us  [on_device(): pl.pallas_call(polarizability_kernel, out_shape=jax.ShapeDtypeStruct((wid...]
    reduce_scatter x2 -> x0, waiting for transfers between devices: 94.8 us -> none  [the longest x1 47.8 us: on_device(): lax.psum_scatter(partial_value.astype(jnp.bfloat16), 'pair', scatter_dime...]
    all_gather x1 -> x0, waiting for transfers between devices: 81.1 us -> none  [on_device(): lax.all_gather(flat_tensor, 'aux', axis=1, tiled=True)]
    another operation x17 -> x0, loops' own time: 78.6 us -> none  [the longest x1 77.9 us: on_device(): lax.map(for_target, jnp.arange(owned_count * lax.axis_size('pair'), dtype...]
    dot_general x21 -> x0, matrix products: 39 us -> none  [the longest x1 16.8 us: on_device(): lax.dot_general(contracted, lax.all_gather(flat_tensor, 'aux', axis=1, ti...]
    dynamic_slice x25 -> x0, local copies, waits for them, and re-layouts: 23.5 us -> none  [the longest x8 11.7 us: pair_term(): active = coupling[source_row, target_row] * coupling[source_col, target_col]]
    dynamic_update_slice x8 -> x0, other arithmetic: 7.81 us -> none  [on_device(): lax.map(for_target, jnp.arange(owned_count * lax.axis_size('pair'), dtype...]
    cond x20 -> x0, local copies, waits for them, and re-layouts: 4.08 us -> none
  transfers between devices with their start and end apart: 3 -> 0, of which waited for: 3 -> 0; matrix products, arithmetic and copies ran while one was open for 0% -> 0% of each run, Pallas kernels for 0% -> 0%
where the time goes in v1:
time: 110 us; the launch traced here: 109 us
  Pallas kernels  106 us (96%)
  other arithmetic  2.79 us (3%)
    pallas_call x1, Pallas kernels, on_device(): pl.pallas_call(polarizability_kernel, out_shape=jax.ShapeDtypeStruct((wid...  106 us
    convert_element_type x1, other arithmetic, on_device(): return part.astype(f32)  2.79 us

profile of v1, /device:TPU:1, one launch (start us, length us, event | category | flops | bytes accessed | tf_op | source)
XLA Modules:
  0.0 108.8 jit_solution(11849102472480048973)
XLA Ops:
  0.0 106.0 %polarizability.1 = bf16[256,2048]{1,0:T(8,128)(2,1)} custom-call(s32[2,8]{1,0:T(2,128)} %pair_ref.1, s32[32,32]{1,0:T(8,128)} %coup_ref.1, bf16[2048,256]{1,0:T(8,128)(2,1)} %bitcast.1, bf16[1024,1024]{1,0:T(8,128)(2,1)} %occ_hbm.1, bf16[1024,1024]{1,0:T(8,128)(2,1)} %virt_hbm.1), custom_call_target="tpu_custom_call" | custom-call | tf_op jit(solution)/shard_map/polarizability/pallas_call | solution.py:319
  106.0 2.8 %convert_element_type.3 = f32[256,2048]{1,0:T(8,128)} convert(bf16[256,2048]{1,0:T(8,128)(2,1)} %polarizability.1) | non-fusion elementwise | flops 524288 | bytes 3145728 | tf_op jit(solution)/shard_map/convert_element_type | solution.py:353

commit v2 on v1

v2 whole, which is shorter than its diff:
```python
import jax
import jax.numpy as jnp
from jax import lax
from jax.experimental import pallas as pl
from jax.experimental.pallas import tpu as pltpu
from jax.sharding import PartitionSpec as P

MESH = pl.DeviceIdType.MESH
RING = 4
CHUNKS = 2
SUBS = 2
Y_OFFSET = (0, 3, 1, 2)


def polarizability_kernel(
    pair_ref, coup_ref, t_hbm, occ_hbm, virt_hbm, o_ref,
    occ, virt, tz, tq, ee, vv, acc, ct, d_send, d_half, d_in, d_own, r_buf,
    send_sem, recv_sem, local_sem,
):
    kdim, width = t_hbm.shape
    chunk = width // CHUNKS
    sub = chunk // SUBS
    block = 32
    square = block * block
    half = kdim // 2
    n_pairs = pair_ref.shape[1]
    owned = n_pairs // RING
    units = range(CHUNKS * SUBS)

    aux = lax.axis_index("aux")
    z = lax.axis_index("pair")
    core = lax.rem(aux, 2)
    y = lax.rem(aux // 2, RING)
    x = aux // (2 * RING)

    def at_x(s):
        return {"aux": (lax.rem(x + s, RING) * RING + y) * 2 + core}

    def at_y(s):
        return {"aux": (x * RING + lax.rem(y + s, RING)) * 2 + core}

    def at_z(s):
        return {"pair": lax.rem(z + s, RING)}

    partner = {"aux": aux + 1 - 2 * core}

    sends = []

    def remote(src, dst, device):
        i = len(sends)
        copy = pltpu.make_async_remote_copy(
            src_ref=src, dst_ref=dst, send_sem=send_sem.at[i], recv_sem=recv_sem.at[i],
            device_id=device, device_id_type=MESH,
        )
        sends.append(copy)
        return copy

    local_counter = [0]

    def local(src, dst):
        i = local_counter[0]
        local_counter[0] += 1
        return pltpu.make_async_copy(src, dst, local_sem.at[i])

    def start(*copies):
        for copy in copies:
            copy.start()

    def arrive(*copies):
        for copy in copies:
            copy.wait_recv()

    mine = tq.at[0, core]
    lo, hi = pl.ds(0, half), pl.ds(half, half)
    halves = (lo, hi)
    cols = [pl.ds(h * chunk, chunk) for h in range(CHUNKS)]
    z_plus = [[remote(mine.at[p, cols[h]], tz.at[h, 0, p], at_z(1)) for p in halves] for h in range(CHUNKS)]
    z_minus = [[remote(mine.at[p, cols[h]], tz.at[h, 1, p], at_z(3)) for p in halves[::-1]] for h in range(CHUNKS)]
    quarters = [pl.ds(i * (half // 2), half // 2) for i in range(4)]
    zf_plus = [[remote(tz.at[h, 0, q], tz.at[h, 2, q], at_z(1)) for q in quarters[:2]] for h in range(CHUNKS)]
    zf_minus = [[remote(tz.at[h, 1, q], tz.at[h, 2, q], at_z(3)) for q in quarters[2:]] for h in range(CHUNKS)]

    x_plus = [remote(mine.at[p], tq.at[3, core, p], at_x(1)) for p in halves]
    x_minus = [remote(mine.at[p], tq.at[1, core, p], at_x(3)) for p in halves[::-1]]
    xf_plus = [remote(tq.at[3, core, q], tq.at[2, core, q], at_x(1)) for q in quarters[:2]]
    xf_minus = [remote(tq.at[1, core, q], tq.at[2, core, q], at_x(3)) for q in quarters[2:]]

    def to_core(o, p):
        return remote(tq.at[o, core, p], tq.at[o, core, p], partner)

    core_own = to_core(0, pl.ds(0, kdim))
    core_plus = [to_core(3, p) for p in halves]
    core_minus = [to_core(1, p) for p in halves[::-1]]
    core_far = [(to_core(2, quarters[q]), to_core(2, quarters[2 + q])) for q in range(2)]

    def yrows(slot, part=0, parts=1):
        return pl.ds(slot * sub + part * (sub // parts), sub // parts)

    y_plus = [remote(ct.at[u, yrows(0)], ct.at[u, yrows(1)], at_y(1)) for u in units]
    y_minus = [remote(ct.at[u, yrows(0)], ct.at[u, yrows(2)], at_y(3)) for u in units]
    yf_plus = [remote(ct.at[u, yrows(1, 0, 2)], ct.at[u, yrows(3, 0, 2)], at_y(1)) for u in units]
    yf_minus = [remote(ct.at[u, yrows(2, 1, 2)], ct.at[u, yrows(3, 1, 2)], at_y(3)) for u in units]

    half_plus = [remote(d_send.at[u, 1, 0], d_half.at[u, 0], at_z(1)) for u in units]
    half_minus = [remote(d_send.at[u, 1, 1], d_half.at[u, 1], at_z(3)) for u in units]
    d_plus = [[remote(d_send.at[u, 0, c], d_in.at[u, 0, c], at_z(1)) for c in range(2)] for u in units]
    d_minus = [[remote(d_send.at[u, 2, c], d_in.at[u, 1, c], at_z(3)) for c in range(2)] for u in units]

    wide = 2 * width
    ocols = pl.ds(pl.multiple_of(y * wide, wide), wide)
    orows = [pl.ds(u * sub, sub) for u in units]
    out_copy = [
        [remote(r_buf.at[u, yrows(s)], o_ref.at[orows[u], ocols], at_y(Y_OFFSET[s])) for s in range(1, RING)]
        for u in units
    ]
    out_own = [local(r_buf.at[u, yrows(0)], o_ref.at[orows[u], ocols]) for u in units]
    keep = local(t_hbm, mine)
    load_occ = local(occ_hbm, occ)
    load_virt = local(virt_hbm, virt)

    start(keep, load_occ, load_virt)

    barrier = pltpu.get_barrier_semaphore()
    greeted = [at_x(1), at_x(3), at_y(1), at_y(2), at_y(3), at_z(1), at_z(3), partner]
    for device in greeted:
        pl.semaphore_signal(barrier, inc=1, device_id=device, device_id_type=MESH)
    pl.semaphore_wait(barrier, len(greeted))

    keep.wait()
    for p in range(2):
        start(z_plus[0][p], z_minus[0][p])
    for p in range(2):
        start(x_plus[p], x_minus[p])
    start(core_own)

    load_occ.wait()
    load_virt.wait()

    def indices(which, positions):
        return [pair_ref[which, position] for position in positions]

    sources = range(n_pairs)
    targets = [z * owned + t for t in range(owned)]

    def onehot(starts, width, step):
        row = lax.broadcasted_iota(jnp.int32, (block, width), 0)
        offset = lax.broadcasted_iota(jnp.int32, (block, width), 1) - row * step
        parts = [(offset == start).astype(jnp.float32).astype(jnp.bfloat16) for start in starts]
        return jnp.concatenate(parts, axis=0)

    def outer(left, right):
        return lax.dot_general(left, right, (((1,), (1,)), ((), ())), preferred_element_type=jnp.float32)

    def select(matrix, which):
        size = matrix.shape[1]
        pick = onehot([i * block for i in indices(which, sources)], size, 1)
        rows = jnp.dot(pick, matrix[...], preferred_element_type=jnp.float32).astype(jnp.bfloat16)
        return outer(onehot([i * block for i in indices(which, targets)], size, 1), rows)

    coupling = coup_ref[...].astype(jnp.float32).astype(jnp.bfloat16)

    def kept(which):
        size = coupling.shape[1]
        pick = onehot(indices(which, sources), size, 0)
        rows = jnp.dot(pick, coupling, preferred_element_type=jnp.float32).astype(jnp.bfloat16)
        return outer(onehot(indices(which, targets), size, 0), rows)

    occ_t = (select(occ, 0) * kept(0) * kept(1)).astype(jnp.bfloat16)
    virt_t = select(virt, 1).astype(jnp.bfloat16)

    def expand(k, carry):
        row = lax.broadcasted_iota(jnp.int32, (n_pairs * block, square), 0)
        lane = lax.broadcasted_iota(jnp.int32, (n_pairs * block, square), 1)
        spread = (row == k * block + lane // block).astype(jnp.float32).astype(jnp.bfloat16)
        tiled = (row == k * block + lane % block).astype(jnp.float32).astype(jnp.bfloat16)
        ee[k] = jnp.dot(occ_t, spread, preferred_element_type=jnp.float32)
        vv[k] = jnp.dot(virt_t, tiled, preferred_element_type=jnp.float32)
        return carry

    lax.fori_loop(0, n_pairs, expand, 0)

    def matrix(k, t, part, lanes):
        left = ee[k, pl.ds(pl.multiple_of(t * block + part * 8, 8), 8), lanes]
        right = vv[k, pl.ds(pl.multiple_of(t * block, block), block), lanes]
        rows = [(left[j : j + 1, :] * right).astype(jnp.bfloat16) for j in range(8)]
        return jnp.concatenate(rows, axis=0)

    def mix(sources, store, lanes=slice(0, square)):
        def step(i, carry):
            t, part = i // 4, lax.rem(i, 4)
            total = None
            for k, load in sources:
                term = jnp.dot(matrix(k, t, part, lanes), load(), preferred_element_type=jnp.float32)
                total = term if total is None else total + term
            store(t, pl.ds(pl.multiple_of(part * 8 * block, 8 * block), 8 * block), total)
            return carry

        lax.fori_loop(0, owned * 4, step, 0)

    def pair(offset, kk):
        return lax.rem(z + offset, RING) * owned + kk

    def store_own(t, rows, total):
        for h in range(CHUNKS):
            acc[h, t, rows, :] = total[:, h * chunk : (h + 1) * chunk]

    def add_to(h):
        def store(t, rows, total):
            acc[h, t, rows, :] += total

        return store

    def arrived(h, slot, kk):
        return lambda: tz[h, slot, kk * half : (kk + 1) * half, :]

    mix([(pair(0, kk), lambda kk=kk: tq[0, core, kk * half : (kk + 1) * half, :]) for kk in range(2)], store_own)

    def mix_near(h, p):
        mix([(pair(3, p), arrived(h, 0, p)), (pair(1, 1 - p), arrived(h, 1, 1 - p))], add_to(h))

    def mix_far(h, q):
        arrive(zf_plus[h][q], zf_minus[h][q])
        size = half // 2
        sources = [
            (pair(2, kk), lambda first=kk * half + q * size: tz[h, 2, first : first + size, :]) for kk in range(2)
        ]
        mix(sources, add_to(h), slice(q * size, (q + 1) * size))

    def finish(h):
        for t in range(owned):
            columns = acc[h, t].T.astype(jnp.bfloat16)
            for v in range(SUBS):
                ct[h * SUBS + v, 0:sub, t * square : (t + 1) * square] = columns[v * sub : (v + 1) * sub]
        start(y_plus[h * SUBS], y_minus[h * SUBS])

    def product(u, r, store):
        o = lax.rem(z + r + RING - x, RING)

        def step(c, carry):
            store(c, jnp.dot(ct[u], tq[o, c], preferred_element_type=jnp.float32))
            return carry

        lax.fori_loop(0, 2, step, 0)

    def product_send(u, r):
        def store(c, value):
            d_send[u, r - 1, c] = value.astype(jnp.bfloat16)

        product(u, r, store)

    def product_own(u):
        def store(c, value):
            d_own[u, c] = value

        product(u, 0, store)

    def product_far(u):
        product_send(u, 2)
        start(half_plus[u], half_minus[u])

    def product_near(u):
        product_send(u, 1)
        start(d_plus[u][1])
        product_send(u, 3)
        start(d_minus[u][0])

    def join(u):
        for copy, r, c, j, onward in ((half_plus[u], 1, 0, 0, d_plus[u][0]), (half_minus[u], 3, 1, 1, d_minus[u][1])):
            arrive(copy)
            total = d_send[u, r - 1, c].astype(jnp.float32) + d_half[u, j].astype(jnp.float32)
            d_send[u, r - 1, c] = total.astype(jnp.bfloat16)
            start(onward)

    def reduce_end(u):
        for c in range(2):
            arrive(d_plus[u][c], d_minus[u][c])
            total = d_own[u, c] + d_in[u, 0, c].astype(jnp.float32) + d_in[u, 1, c].astype(jnp.float32)
            r_buf[u, :, c * width : (c + 1) * width] = total.astype(jnp.bfloat16)
        start(*out_copy[u])
        start(out_own[u])

    def y_pass(u):
        arrive(y_plus[u])
        start(yf_plus[u])
        arrive(y_minus[u])
        start(yf_minus[u])
        if u % SUBS < SUBS - 1:
            start(y_plus[u + 1], y_minus[u + 1])

    def z_pass(h):
        arrive(z_plus[h][0])
        start(*zf_plus[h])
        arrive(z_minus[h][0])
        start(*zf_minus[h])

    z_pass(0)
    for p in range(2):
        start(z_plus[1][p], z_minus[1][p])
    mix_near(0, 0)
    arrive(x_plus[0])
    start(*xf_plus, core_plus[0])
    arrive(x_minus[0])
    start(*xf_minus, core_minus[0])
    arrive(z_plus[0][1], z_minus[0][1])
    mix_near(0, 1)
    mix_far(0, 0)
    mix_far(0, 1)
    finish(0)
    z_pass(1)
    arrive(x_plus[1], x_minus[1])
    start(core_plus[1], core_minus[1])
    mix_near(1, 0)
    y_pass(0)
    arrive(z_plus[1][1], z_minus[1][1])
    mix_near(1, 1)
    arrive(xf_plus[0], xf_minus[0])
    start(*core_far[0])
    mix_far(1, 0)
    arrive(xf_plus[1], xf_minus[1])
    start(*core_far[1])
    arrive(yf_plus[0], yf_minus[0])
    y_pass(1)
    arrive(core_own, *core_plus, *core_minus, *core_far[0], *core_far[1])
    product_far(0)
    mix_far(1, 1)
    finish(1)
    product_near(0)
    join(0)
    arrive(yf_plus[1], yf_minus[1])
    product_far(1)
    product_near(1)
    y_pass(2)
    join(1)
    product_own(0)
    product_own(1)
    arrive(yf_plus[2], yf_minus[2])
    product_far(2)
    product_near(2)
    y_pass(3)
    join(2)
    reduce_end(0)
    product_own(2)
    reduce_end(1)
    arrive(yf_plus[3], yf_minus[3])
    product_far(3)
    product_near(3)
    join(3)
    product_own(3)
    reduce_end(2)
    reduce_end(3)

    for u in units:
        arrive(*out_copy[u])
        out_own[u].wait()
    for copy in sends:
        copy.wait_send()


def on_device(three_center, pair_index, green_occ, green_virt, coupling):
    owned, block, _, width = three_center.shape
    kdim = owned * block * block
    chunk = width // CHUNKS
    sub = chunk // SUBS
    units = CHUNKS * SUBS
    rows = RING * sub
    n_pairs = pair_index.shape[1]
    bf16, f32 = jnp.bfloat16, jnp.float32
    part = pl.pallas_call(
        polarizability_kernel,
        out_shape=jax.ShapeDtypeStruct((width, RING * 2 * width), bf16),
        in_specs=[
            pl.BlockSpec(memory_space=pltpu.SMEM),
            pl.BlockSpec(memory_space=pltpu.VMEM),
            pl.BlockSpec(memory_space=pl.ANY),
            pl.BlockSpec(memory_space=pl.ANY),
            pl.BlockSpec(memory_space=pl.ANY),
        ],
        out_specs=pl.BlockSpec(memory_space=pl.ANY),
        scratch_shapes=[
            pltpu.VMEM(green_occ.shape, bf16),
            pltpu.VMEM(green_virt.shape, bf16),
            pltpu.VMEM((CHUNKS, 3, kdim, chunk), bf16),
            pltpu.VMEM((RING, 2, kdim, width), bf16),
            pltpu.VMEM((n_pairs, owned * block, block * block), f32),
            pltpu.VMEM((n_pairs, owned * block, block * block), f32),
            pltpu.VMEM((CHUNKS, owned, block * block, chunk), f32),
            pltpu.VMEM((units, rows, kdim), bf16),
            pltpu.VMEM((units, 3, 2, rows, width), bf16),
            pltpu.VMEM((units, 2, rows, width), bf16),
            pltpu.VMEM((units, 2, 2, rows, width), bf16),
            pltpu.VMEM((units, 2, rows, width), f32),
            pltpu.VMEM((units, rows, 2 * width), bf16),
            pltpu.SemaphoreType.DMA((96,)),
            pltpu.SemaphoreType.DMA((96,)),
            pltpu.SemaphoreType.DMA((8,)),
        ],
        compiler_params=pltpu.CompilerParams(
            collective_id=0, has_side_effects=True, vmem_limit_bytes=56 * 1024 * 1024
        ),
        name="polarizability",
    )(pair_index, coupling, three_center.reshape(kdim, width), green_occ, green_virt)
    return part.astype(f32)


def solution(mesh):
    placed = (P("pair", None, None, "aux"), P(), P(), P(), P())
    return jax.shard_map(
        on_device, mesh=mesh, in_specs=placed, out_specs=P("aux", "pair"), check_vma=False
    )
```

time: 110 us -> 95.7 us (0.87)
  Pallas kernels: 106 us -> 92.7 us
    pallas_call x1, Pallas kernels: 106 us -> 92.7 us  [on_device(): pl.pallas_call(polarizability_kernel, out_shape=jax.ShapeDtypeStruct((wid...]
where the time goes in v2:
time: 95.7 us; the launch traced here: 95.5 us
  Pallas kernels  92.7 us (97%)
  other arithmetic  2.79 us (3%)
    pallas_call x1, Pallas kernels, on_device(): pl.pallas_call(polarizability_kernel, out_shape=jax.ShapeDtypeStruct((wid...  92.7 us
    convert_element_type x1, other arithmetic, on_device(): return part.astype(f32)  2.79 us

profile of v2, /device:TPU:1, one launch (start us, length us, event | category | flops | bytes accessed | tf_op | source)
XLA Modules:
  0.0 95.5 jit_solution(2032275657748899508)
XLA Ops:
  0.0 92.7 %polarizability.1 = bf16[256,2048]{1,0:T(8,128)(2,1)} custom-call(s32[2,8]{1,0:T(2,128)} %pair_ref.1, s32[32,32]{1,0:T(8,128)} %coup_ref.1, bf16[2048,256]{1,0:T(8,128)(2,1)} %bitcast.1, bf16[1024,1024]{1,0:T(8,128)(2,1)} %occ_hbm.1, bf16[1024,1024]{1,0:T(8,128)(2,1)} %virt_hbm.1), custom_call_target="tpu_custom_call" | custom-call | tf_op jit(solution)/shard_map/polarizability/pallas_call | solution.py:368
  92.7 2.8 %convert_element_type.3 = f32[256,2048]{1,0:T(8,128)} convert(bf16[256,2048]{1,0:T(8,128)(2,1)} %polarizability.1) | non-fusion elementwise | flops 524288 | bytes 3145728 | tf_op jit(solution)/shard_map/convert_element_type | solution.py:402

commit v3 on v2

--- a/solution.py
+++ b/solution.py
@@ -96,8 +96,8 @@
     def yrows(slot, part=0, parts=1):
         return pl.ds(slot * sub + part * (sub // parts), sub // parts)
 
-    y_plus = [remote(ct.at[u, yrows(0)], ct.at[u, yrows(1)], at_y(1)) for u in units]
-    y_minus = [remote(ct.at[u, yrows(0)], ct.at[u, yrows(2)], at_y(3)) for u in units]
+    y_plus = [[remote(ct.at[u, yrows(0, i, 2)], ct.at[u, yrows(1, i, 2)], at_y(1)) for i in (0, 1)] for u in units]
+    y_minus = [[remote(ct.at[u, yrows(0, i, 2)], ct.at[u, yrows(2, i, 2)], at_y(3)) for i in (1, 0)] for u in units]
     yf_plus = [remote(ct.at[u, yrows(1, 0, 2)], ct.at[u, yrows(3, 0, 2)], at_y(1)) for u in units]
     yf_minus = [remote(ct.at[u, yrows(2, 1, 2)], ct.at[u, yrows(3, 1, 2)], at_y(3)) for u in units]
 
@@ -226,14 +226,20 @@
         ]
         mix(sources, add_to(h), slice(q * size, (q + 1) * size))
 
+    def y_send(u):
+        for p in range(2):
+            start(y_plus[u][p], y_minus[u][p])
+
     def finish(h):
         for t in range(owned):
             columns = acc[h, t].T.astype(jnp.bfloat16)
             for v in range(SUBS):
                 ct[h * SUBS + v, 0:sub, t * square : (t + 1) * square] = columns[v * sub : (v + 1) * sub]
-        start(y_plus[h * SUBS], y_minus[h * SUBS])
+        y_send(h * SUBS)
 
     def product(u, r, store):
+        if u == 0:
+            far_block(r)
         o = lax.rem(z + r + RING - x, RING)
 
         def step(c, carry):
@@ -280,12 +286,23 @@
         start(out_own[u])
 
     def y_pass(u):
-        arrive(y_plus[u])
+        arrive(y_plus[u][0])
         start(yf_plus[u])
-        arrive(y_minus[u])
+        arrive(y_minus[u][0])
         start(yf_minus[u])
         if u % SUBS < SUBS - 1:
-            start(y_plus[u + 1], y_minus[u + 1])
+            y_send(u + 1)
+
+    def y_arrive(u):
+        arrive(y_plus[u][1], y_minus[u][1], yf_plus[u], yf_minus[u])
+
+    def far_block(r):
+        @pl.when(lax.rem(z + r + RING - x, RING) == 2)
+        def _():
+            for q in range(2):
+                arrive(xf_plus[q], xf_minus[q])
+                start(*core_far[q])
+            arrive(*core_far[0], *core_far[1])
 
     def z_pass(h):
         arrive(z_plus[h][0])
@@ -313,27 +330,23 @@
     y_pass(0)
     arrive(z_plus[1][1], z_minus[1][1])
     mix_near(1, 1)
-    arrive(xf_plus[0], xf_minus[0])
-    start(*core_far[0])
+    y_arrive(0)
+    arrive(core_own, *core_plus, *core_minus)
+    product_far(0)
     mix_far(1, 0)
-    arrive(xf_plus[1], xf_minus[1])
-    start(*core_far[1])
-    arrive(yf_plus[0], yf_minus[0])
+    product_near(0)
     y_pass(1)
-    arrive(core_own, *core_plus, *core_minus, *core_far[0], *core_far[1])
-    product_far(0)
     mix_far(1, 1)
     finish(1)
-    product_near(0)
     join(0)
-    arrive(yf_plus[1], yf_minus[1])
+    y_arrive(1)
     product_far(1)
+    y_pass(2)
     product_near(1)
-    y_pass(2)
     join(1)
     product_own(0)
     product_own(1)
-    arrive(yf_plus[2], yf_minus[2])
+    y_arrive(2)
     product_far(2)
     product_near(2)
     y_pass(3)
@@ -341,7 +354,7 @@
     reduce_end(0)
     product_own(2)
     reduce_end(1)
-    arrive(yf_plus[3], yf_minus[3])
+    y_arrive(3)
     product_far(3)
     product_near(3)
     join(3)

time: 95.7 us -> 93.9 us (0.981)
  Pallas kernels: 92.7 us -> 91 us
    pallas_call x1, Pallas kernels: 92.7 us -> 91 us  [on_device(): pl.pallas_call(polarizability_kernel, out_shape=jax.ShapeDtypeStruct((wid...]
where the time goes in v3:
time: 93.9 us; the launch traced here: 93.8 us
  Pallas kernels  91 us (97%)
  other arithmetic  2.79 us (3%)
    pallas_call x1, Pallas kernels, on_device(): pl.pallas_call(polarizability_kernel, out_shape=jax.ShapeDtypeStruct((wid...  91 us
    convert_element_type x1, other arithmetic, on_device(): return part.astype(f32)  2.79 us

profile of v3, /device:TPU:1, one launch (start us, length us, event | category | flops | bytes accessed | tf_op | source)
XLA Modules:
  0.0 93.8 jit_solution(10195960486463666432)
XLA Ops:
  0.0 91.0 %polarizability.1 = bf16[256,2048]{1,0:T(8,128)(2,1)} custom-call(s32[2,8]{1,0:T(2,128)} %pair_ref.1, s32[32,32]{1,0:T(8,128)} %coup_ref.1, bf16[2048,256]{1,0:T(8,128)(2,1)} %bitcast.1, bf16[1024,1024]{1,0:T(8,128)(2,1)} %occ_hbm.1, bf16[1024,1024]{1,0:T(8,128)(2,1)} %virt_hbm.1), custom_call_target="tpu_custom_call" | custom-call | tf_op jit(solution)/shard_map/polarizability/pallas_call | solution.py:381
  91.0 2.8 %convert_element_type.3 = f32[256,2048]{1,0:T(8,128)} convert(bf16[256,2048]{1,0:T(8,128)(2,1)} %polarizability.1) | non-fusion elementwise | flops 524288 | bytes 3145728 | tf_op jit(solution)/shard_map/convert_element_type | solution.py:415

commit v4 on v3

--- a/solution.py
+++ b/solution.py
@@ -333,9 +333,9 @@
     y_arrive(0)
     arrive(core_own, *core_plus, *core_minus)
     product_far(0)
-    mix_far(1, 0)
     product_near(0)
     y_pass(1)
+    mix_far(1, 0)
     mix_far(1, 1)
     finish(1)
     join(0)
@@ -357,9 +357,9 @@
     y_arrive(3)
     product_far(3)
     product_near(3)
+    reduce_end(2)
     join(3)
     product_own(3)
-    reduce_end(2)
     reduce_end(3)
 
     for u in units:

time: 93.9 us -> 93.2 us (level)
  no operation moved by 1% of the time
where the time goes in v4:
time: 93.2 us; the launch traced here: 93 us
  Pallas kernels  90.2 us (97%)
  other arithmetic  2.79 us (3%)
    pallas_call x1, Pallas kernels, on_device(): pl.pallas_call(polarizability_kernel, out_shape=jax.ShapeDtypeStruct((wid...  90.2 us
    convert_element_type x1, other arithmetic, on_device(): return part.astype(f32)  2.79 us

profile of v4, /device:TPU:1, one launch (start us, length us, event | category | flops | bytes accessed | tf_op | source)
XLA Modules:
  0.0 93.0 jit_solution(2903755169363507032)
XLA Ops:
  0.0 90.2 %polarizability.1 = bf16[256,2048]{1,0:T(8,128)(2,1)} custom-call(s32[2,8]{1,0:T(2,128)} %pair_ref.1, s32[32,32]{1,0:T(8,128)} %coup_ref.1, bf16[2048,256]{1,0:T(8,128)(2,1)} %bitcast.1, bf16[1024,1024]{1,0:T(8,128)(2,1)} %occ_hbm.1, bf16[1024,1024]{1,0:T(8,128)(2,1)} %virt_hbm.1), custom_call_target="tpu_custom_call" | custom-call | tf_op jit(solution)/shard_map/polarizability/pallas_call | solution.py:381
  90.2 2.8 %convert_element_type.3 = f32[256,2048]{1,0:T(8,128)} convert(bf16[256,2048]{1,0:T(8,128)(2,1)} %polarizability.1) | non-fusion elementwise | flops 524288 | bytes 3145728 | tf_op jit(solution)/shard_map/convert_element_type | solution.py:415

commit v5 on v4

--- a/solution.py
+++ b/solution.py
@@ -124,9 +124,8 @@
     greeted = [at_x(1), at_x(3), at_y(1), at_y(2), at_y(3), at_z(1), at_z(3), partner]
     for device in greeted:
         pl.semaphore_signal(barrier, inc=1, device_id=device, device_id_type=MESH)
+    keep.wait()
     pl.semaphore_wait(barrier, len(greeted))
-
-    keep.wait()
     for p in range(2):
         start(z_plus[0][p], z_minus[0][p])
     for p in range(2):
@@ -351,14 +350,14 @@
     product_near(2)
     y_pass(3)
     join(2)
-    reduce_end(0)
-    product_own(2)
-    reduce_end(1)
     y_arrive(3)
     product_far(3)
+    reduce_end(0)
     product_near(3)
+    reduce_end(1)
+    product_own(2)
+    join(3)
     reduce_end(2)
-    join(3)
     product_own(3)
     reduce_end(3)
 

time: 93.2 us -> 93.1 us (level)
  no operation moved by 1% of the time
where the time goes in v5:
time: 93.1 us; the launch traced here: 93 us
  Pallas kernels  90.2 us (97%)
  other arithmetic  2.79 us (3%)
    pallas_call x1, Pallas kernels, on_device(): pl.pallas_call(polarizability_kernel, out_shape=jax.ShapeDtypeStruct((wid...  90.2 us
    convert_element_type x1, other arithmetic, on_device(): return part.astype(f32)  2.79 us

profile of v5, /device:TPU:1, one launch (start us, length us, event | category | flops | bytes accessed | tf_op | source)
XLA Modules:
  0.0 93.0 jit_solution(9401594142391225600)
XLA Ops:
  0.0 90.2 %polarizability.1 = bf16[256,2048]{1,0:T(8,128)(2,1)} custom-call(s32[2,8]{1,0:T(2,128)} %pair_ref.1, s32[32,32]{1,0:T(8,128)} %coup_ref.1, bf16[2048,256]{1,0:T(8,128)(2,1)} %bitcast.1, bf16[1024,1024]{1,0:T(8,128)(2,1)} %occ_hbm.1, bf16[1024,1024]{1,0:T(8,128)(2,1)} %virt_hbm.1), custom_call_target="tpu_custom_call" | custom-call | tf_op jit(solution)/shard_map/polarizability/pallas_call | solution.py:380
  90.2 2.8 %convert_element_type.3 = f32[256,2048]{1,0:T(8,128)} convert(bf16[256,2048]{1,0:T(8,128)(2,1)} %polarizability.1) | non-fusion elementwise | flops 524288 | bytes 3145728 | tf_op jit(solution)/shard_map/convert_element_type | solution.py:414
